TPU v7x, 256 devices: a whole 4x4x8 slice. The times are simulated.
256 devices in a mesh: pipe: 4 (over y), tensor: 32 (over x, z_hi, core), dp: 2 (over z_lo).
Axes of the slice: x: 4, y: 4, z: 8 (z_hi: 4, z_lo: 2; z = z_hi * 2 + z_lo), core: 2. Of those that a mesh axis runs over, the one named last changes fastest.
Arguments:
- weight_main: bfloat16 [4, 4096, 2, 8192], P('pipe', None, None, 'tensor'), may hold values from -0.09375 to 0.09375
- weight_state: bfloat16 [4, 4096, 2, 1024], P('pipe', None, None, 'tensor'), may hold values from -0.09375 to 0.09375
- weight_step: bfloat16 [4, 128, 4096], P('pipe', 'tensor'), may hold values from -0.09375 to 0.09375
- weight_out: bfloat16 [4, 8192, 4096], P('pipe', 'tensor'), may hold values from -0.0625 to 0.0625
- conv_main: float32 [4, 4, 8192], P('pipe', None, 'tensor'), may hold values from -3 to 3
- conv_state: float32 [4, 4, 2, 1024], P('pipe'), may hold values from -3 to 3
- step_bias: float32 [4, 128], P('pipe', 'tensor'), may hold values from -3 to 0
- decay_log: float32 [4, 128], P('pipe', 'tensor'), may hold values from -5 to 0.5
- skip_gain: float32 [4, 128], P('pipe', 'tensor'), may hold values from 1 to 6
- norm_gain: float32 [4, 8192], P('pipe', 'tensor'), may hold values from 0.5 to 1.5
- saved_main: bfloat16 [4, 256, 2, 8192], P('pipe', 'dp', None, 'tensor'), parts along dimension 1, may hold values from -6 to 6
- saved_state: bfloat16 [4, 256, 2, 1024], P('pipe', 'dp'), parts along dimension 1, may hold values from -6 to 6
- saved_step: bfloat16 [4, 128, 256], P('pipe', 'tensor', 'dp'), parts along dimension 2, may hold values from -6 to 6
- output_grad: bfloat16 [256, 4096], P('dp', 'tensor'), parts along dimension 0, may hold values from -6 to 6
Outputs:
- input_grads: bfloat16 [4, 256, 4096], P('pipe', 'dp', 'tensor'), parts along dimension 1
There are 2 independent parts, one for each index of `dp`. A program takes and returns all parts, laid end to end along the dimension named above; an argument that names none is the same for every part. Nothing has to cross between parts.
All inputs are finite; a program needn't handle non-finite values.
Results may differ from a plain program's by a relative error of at most 0.02.
Values may be sent and summed in bfloat16 or wider, within the bound.
A program may use at most 64 MiB of HBM per device.

v0:
```python
import jax
import jax.numpy as jnp
from jax import lax
from jax.sharding import PartitionSpec as P

NSTATE = 128
GROUP_SPAN = 4
STRETCH = 128
EPSILON = 1e-05
HIGHEST = lax.Precision.HIGHEST


def from_partner(value, axis, bit):
    mask = 2**bit
    pairs = [(source, source ^ mask) for source in range(lax.axis_size(axis))]
    return lax.ppermute(value, axis, pairs)


def passed_along(value, axis, steps):
    count = lax.axis_size(axis)
    leading, last = (max(0, -steps), min(count, count - steps))
    return lax.ppermute(value, axis, [(source, source + steps) for source in range(leading, last)])


def causal_conv(signal, kernel):
    taps = kernel.shape[0]
    length = signal.shape[0]
    padded = jnp.pad(signal, ((taps - 1, 0), (0, 0)))
    summed = kernel[0] * padded[0:length]
    for offset in range(1, taps):
        summed = summed + kernel[offset] * padded[offset : offset + length]
    return summed


def state_space(values, step_sizes, decay_rates, inputs, readout):
    length, head_count, head_size = values.shape
    blocks = length // STRETCH
    state_width = inputs.shape[1]
    decays = (step_sizes * decay_rates[:, None]).reshape(head_count, blocks, STRETCH)
    running = jnp.cumsum(decays, axis=2)
    scaled = (values * step_sizes.T[:, :, None]).reshape(blocks, STRETCH, head_count, head_size)
    inputs_blocked = inputs.reshape(blocks, STRETCH, state_width)
    readout_blocked = readout.reshape(blocks, STRETCH, state_width)
    scores = jnp.einsum("cin,cjn->cij", readout_blocked, inputs_blocked, precision=HIGHEST)
    position = jnp.arange(STRETCH)
    causal = position[:, None] >= position[None, :]
    differ = running[:, :, :, None] - running[:, :, None, :]
    weights = jnp.where(causal, jnp.exp(jnp.where(causal, differ, 0.0)), 0.0) * scores[None]
    within = jnp.einsum("hcij,cjhp->cihp", weights, scaled, precision=HIGHEST)
    tail_decay = jnp.exp(running[:, :, -1:] - running)
    weighted = scaled * jnp.transpose(tail_decay, (1, 2, 0))[:, :, :, None]
    block_sums = jnp.einsum("cjhp,cjn->chpn", weighted, inputs_blocked, precision=HIGHEST)
    shrinks = jnp.exp(running[:, :, -1]).T

    def advance(carried, item):
        newest, shrink = item
        return (carried * shrink[:, None, None] + newest, carried)

    anchor = jnp.zeros((head_count, head_size, state_width), jnp.float32)
    _, entering = lax.scan(advance, anchor, (block_sums, shrinks))
    across = jnp.einsum("cin,chpn->cihp", readout_blocked, entering, precision=HIGHEST)
    across = across * jnp.transpose(jnp.exp(running), (1, 2, 0))[:, :, :, None]
    return (within + across).reshape(length, head_count, head_size)


def mamba_mixer(
    main_proj,
    state_proj,
    step_proj,
    conv_main,
    conv_state,
    step_bias,
    decay_log,
    skip_gain,
    norm_gain,
):
    length = main_proj.shape[0]
    head_count = step_proj.shape[0]
    gating = main_proj[:, 0]
    mixed_in = jax.nn.silu(causal_conv(main_proj[:, 1], conv_main))
    flat_state = state_proj.reshape(length, -1)
    state_conv = jax.nn.silu(
        causal_conv(flat_state, conv_state.reshape(conv_state.shape[0], -1))
    ).reshape(length, 2, -1)
    step_sizes = jax.nn.softplus(step_proj + step_bias[:, None])
    decay_rates = -jnp.exp(decay_log)
    values = mixed_in.reshape(length, head_count, -1)
    scanned = state_space(values, step_sizes, decay_rates, state_conv[:, 0], state_conv[:, 1])
    scanned = scanned + skip_gain[None, :, None] * values
    gated = scanned.reshape(length, -1) * jax.nn.silu(gating)
    inverse = lax.rsqrt(jnp.mean(gated * gated, axis=1, keepdims=True) + EPSILON)
    return gated * inverse * norm_gain


def body(
    weight_main,
    weight_state,
    weight_step,
    weight_out,
    conv_main,
    conv_state,
    step_bias,
    decay_log,
    skip_gain,
    norm_gain,
    saved_main,
    saved_state,
    saved_step,
    output_grad,
):
    sections = lax.axis_size("pipe")
    section = lax.axis_index("pipe")
    tensor_index = lax.axis_index("tensor")
    member = tensor_index % GROUP_SPAN
    group = tensor_index // GROUP_SPAN
    span_bits = GROUP_SPAN.bit_length() - 1
    length = saved_main.shape[1]
    col_count = output_grad.shape[1]
    model_width = weight_out.shape[2]
    main_cols = weight_main[0].reshape(model_width, -1)
    state_cols = weight_state[0].reshape(model_width, -1)
    step_rows = weight_step[0]
    out_rows = weight_out[0]
    state_group = lax.dynamic_slice_in_dim(saved_state[0], group * NSTATE, NSTATE, 2)
    conv_group = lax.dynamic_slice_in_dim(conv_state[0], group * NSTATE, NSTATE, 2)

    def local_mixer(first_in, second_in, third_in):
        return mamba_mixer(
            first_in,
            second_in,
            third_in,
            conv_main[0],
            conv_group,
            step_bias[0],
            decay_log[0],
            skip_gain[0],
            norm_gain[0],
        )

    _, pullback = jax.vjp(
        local_mixer,
        saved_main[0].astype(jnp.float32),
        state_group.astype(jnp.float32),
        saved_step[0].astype(jnp.float32),
    )
    result = jnp.zeros((length, col_count), jnp.bfloat16)
    incoming = output_grad
    for moment in range(sections):
        back_grad_main, back_grad_state, back_grad_step = pullback(
            lax.dot_general(
                lax.all_gather(incoming, "tensor", axis=1, tiled=True),
                out_rows,
                (((1,), (1,)), ((), ())),
                preferred_element_type=jnp.float32,
            )
        )
        kept = back_grad_state
        for bit in range(span_bits - 1, -1, -1):
            half = kept.shape[2] // 2
            lower = kept[:, :, :half]
            upper = kept[:, :, half:]
            high = member // 2**bit % 2 == 1
            own = jnp.where(high, upper, lower)
            other = jnp.where(high, lower, upper)
            kept = own + from_partner(other, "tensor", bit)
        grad_main = back_grad_main.astype(jnp.bfloat16).reshape(length, -1)
        grad_state = kept.astype(jnp.bfloat16).reshape(length, -1)
        grad_step = back_grad_step.astype(jnp.bfloat16)
        summed = lax.dot_general(
            main_cols, grad_main, (((1,), (1,)), ((), ())), preferred_element_type=jnp.float32
        )
        summed = summed + lax.dot_general(
            state_cols, grad_state, (((1,), (1,)), ((), ())), preferred_element_type=jnp.float32
        )
        owned = lax.psum_scatter(
            summed
            + lax.dot_general(
                step_rows, grad_step, (((0,), (0,)), ((), ())), preferred_element_type=jnp.float32
            ),
            "tensor",
            scatter_dimension=0,
            tiled=True,
        ).T.astype(jnp.bfloat16)
        result = jnp.where(section == sections - 1 - moment, owned, result)
        if moment + 1 < sections:
            incoming = passed_along(owned, "pipe", -1)
    return result[None]


def solution(mesh):
    return jax.shard_map(
        body,
        mesh=mesh,
        in_specs=(
            P("pipe", None, None, "tensor"),
            P("pipe", None, None, "tensor"),
            P("pipe", "tensor", None),
            P("pipe", "tensor", None),
            P("pipe", None, "tensor"),
            P("pipe", None, None, None),
            P("pipe", "tensor"),
            P("pipe", "tensor"),
            P("pipe", "tensor"),
            P("pipe", "tensor"),
            P("pipe", "dp", None, "tensor"),
            P("pipe", "dp", None, None),
            P("pipe", "tensor", "dp"),
            P("dp", "tensor"),
        ),
        out_specs=P("pipe", "dp", "tensor"),
        check_vma=False,
    )
```

profile of v0, /device:TPU:8, one launch (start us, length us, event | category | flops | bytes accessed | tf_op | source)
XLA Modules:
  0.0 773.3 jit_solution(89910686781437993)
XLA Ops:
  20.5 4.9 copy.113
  25.4 39.5 %all-gather.5.cloned.1.call-done = bf16[128,4096]{1,0:T(8,128)(2,1)} async-done(((bf16[128,128]{1,0:T(8,128)(2,1)}), bf16[128,4096]{1,0:T(8,128)(2,1)}) %all-gather.5.cloned.1.call-update) | async-done | bytes 1048592 | tf_op jit(solution)/shard_map/all_gather | solution.py:151
  69.2 2.3 fusion.49
  72.1 2.8 fusion.63
  90.2 5.2 fusion.193
  98.2 2.5 reduce_window_sum.50
  105.7 89.8 %reduce-scatter.5.cloned.1.call-done = f32[128,128]{0,1:T(8,128)} async-done(((f32[4096,128]{0,1:T(8,128)}), f32[128,128]{0,1:T(8,128)}) %reduce-scatter.5.cloned.1.call-update) | async-done | bytes 65552 | tf_op jit(solution)/shard_map/reduce_scatter | solution.py:175
  196.3 2.4 collective-permute-start.2
  198.8 3.5 collective-permute-done.2
  202.5 49.6 %all-gather.7.cloned.1.call-done = bf16[128,4096]{1,0:T(8,128)(2,1)} async-done(((bf16[128,128]{1,0:T(8,128)(2,1)}), bf16[128,4096]{1,0:T(8,128)(2,1)}) %all-gather.7.cloned.1.call-update) | async-done | bytes 1048592 | tf_op jit(solution)/shard_map/all_gather | solution.py:151
  252.1 2.2 multiply_reduce_fusion.9
  258.1 2.3 fusion.51
  260.5 2.8 fusion.62
  284.8 5.2 fusion.194
  292.8 2.5 reduce_window_sum.52
  300.3 90.0 %reduce-scatter.7.cloned.1.call-done = f32[128,128]{0,1:T(8,128)} async-done(((f32[4096,128]{0,1:T(8,128)}), f32[128,128]{0,1:T(8,128)}) %reduce-scatter.7.cloned.1.call-update) | async-done | bytes 65552 | tf_op jit(solution)/shard_map/reduce_scatter | solution.py:175
  391.1 2.4 collective-permute-start.5
  393.6 3.5 collective-permute-done.5
  397.1 49.8 %all-gather.9.cloned.1.call-done = bf16[128,4096]{1,0:T(8,128)(2,1)} async-done(((bf16[128,128]{1,0:T(8,128)(2,1)}), bf16[128,4096]{1,0:T(8,128)(2,1)}) %all-gather.9.cloned.1.call-update) | async-done | bytes 1048592 | tf_op jit(solution)/shard_map/all_gather | solution.py:151
  446.9 2.2 multiply_reduce_fusion.7
  452.9 2.3 fusion.53
  455.3 2.8 fusion.61
  479.5 5.2 fusion.195
  487.5 2.5 reduce_window_sum.54
  495.0 89.9 %reduce-scatter.9.cloned.1.call-done = f32[128,128]{0,1:T(8,128)} async-done(((f32[4096,128]{0,1:T(8,128)}), f32[128,128]{0,1:T(8,128)}) %reduce-scatter.9.cloned.1.call-update) | async-done | bytes 65552 | tf_op jit(solution)/shard_map/reduce_scatter | solution.py:175
  585.8 2.4 collective-permute-start.8
  588.2 3.5 collective-permute-done.8
  591.8 49.8 %all-gather.11.cloned.1.call-done = bf16[128,4096]{1,0:T(8,128)(2,1)} async-done(((bf16[128,128]{1,0:T(8,128)(2,1)}), bf16[128,4096]{1,0:T(8,128)(2,1)}) %all-gather.11.cloned.1.call-update) | async-done | bytes 1048592 | tf_op jit(solution)/shard_map/all_gather | solution.py:151
  647.0 2.3 fusion.55
  649.3 2.7 fusion.60
  663.3 5.1 fusion.196
  674.9 90.1 %reduce-scatter.11.cloned.1.call-done = f32[128,128]{0,1:T(8,128)} async-done(((f32[4096,128]{0,1:T(8,128)}), f32[128,128]{0,1:T(8,128)}) %reduce-scatter.11.cloned.1.call-update) | async-done | bytes 65552 | tf_op jit(solution)/shard_map/reduce_scatter | solution.py:175
  (359 shorter events, 134.3 us)
Async XLA Ops:
  6.5 58.3 %copy-start = (bf16[1,256,4096]{2,1,0:T(8,128)(2,1)S(1)}, bf16[1,256,4096]{2,1,0:T(8,128)(2,1)}, u32[]{:S(2)}) copy-start(bf16[1,256,4096]{2,1,0:T(8,128)(2,1)} %param.17) | copy-start | bytes 6291460
  6.5 58.3 %all-gather.5.cloned.1.call-start = ((), (), s32[]{:S(2)}) async-start(), calls=%async_computation.4 | async-start | bytes 1081344 | tf_op jit(solution)/shard_map/all_gather | solution.py:151
  7.3 188.2 %reduce-scatter.5.cloned.1.call-start = ((), (), s32[]{:S(2)}) async-start(), calls=%async_computation.5 | async-start | bytes 2162688 | tf_op jit(solution)/shard_map/reduce_scatter | solution.py:175
  8.3 8.3 %copy-start.85 = (f32[1,4]{1,0:T(1,128)S(1)}, f32[1,4]{1,0:T(1,128)}, u32[]{:S(2)}) copy-start(f32[1,4]{1,0:T(1,128)} %param.22) | copy-start | bytes 52
  11.1 56.5 %copy-start.2 = (f32[128,2,256]{2,0,1:T(8,128)}, f32[128,2,256]{2,0,1:T(8,128)S(1)}, u32[]{:S(2)}) copy-start(f32[128,2,256]{2,0,1:T(8,128)S(1)} %bitcast_convert_fusion) | copy-start | bytes 786436
  11.3 14.1 %copy-start.31 = (f32[128,256]{0,1:T(8,128)}, f32[128,256]{0,1:T(8,128)S(1)}, u32[]{:S(2)}) copy-start(f32[128,256]{0,1:T(8,128)S(1)} %copy.52) | copy-start | bytes 393220
  67.0 11.3 %copy-start.6 = (f32[128,256]{1,0:T(8,128)}, f32[128,256]{1,0:T(8,128)S(1)}, u32[]{:S(2)}) copy-start(f32[128,256]{1,0:T(8,128)S(1)} %get-tuple-element.152) | copy-start | bytes 393220
  68.4 11.2 %copy-start.25 = (f32[128,256]{1,0:T(8,128)S(1)}, f32[128,256]{1,0:T(8,128)}, u32[]{:S(2)}) copy-start(f32[128,256]{1,0:T(8,128)} %get-tuple-element.145) | copy-start | bytes 393220
  78.3 7.6 copy-start.40
  78.3 7.6 copy-start.42
  84.8 10.7 %collective-permute-start = (f32[128,2,64]{0,2,1:T(8,128)}, f32[128,2,64]{0,2,1:T(8,128)}, u32[]{:S(2)}, u32[]{:S(2)}) collective-permute-start(f32[128,2,64]{0,2,1:T(8,128)} %slice_select_fusion.3), channel_id=1, source_target_pairs={{0,4},{2,6},{4,0},{6,2},{8,12},{10,14},{12,8},{14,10},{16,20},{18,... | collective-permute-start | bytes 196616 | tf_op jit(solution)/shard_map/ppermute | solution.py:16
  90.2 11.3 %copy-start.1 = (bf16[1,4096,2,32]{1,3,2,0:T(8,128)(2,1)S(1)}, bf16[1,4096,2,32]{1,3,2,0:T(8,128)(2,1)}, u32[]{:S(2)}) copy-start(bf16[1,4096,2,32]{1,3,2,0:T(8,128)(2,1)} %param.15) | copy-start | bytes 1572868
  97.5 3.2 collective-permute-start.1
  105.7 146.4 %all-gather.7.cloned.1.call-start = ((), (), s32[]{:S(2)}) async-start(), calls=%async_computation.6 | async-start | bytes 1081344 | tf_op jit(solution)/shard_map/all_gather | solution.py:151
  196.3 5.9 collective-permute-start.2
  202.3 188.0 %reduce-scatter.7.cloned.1.call-start = ((), (), s32[]{:S(2)}) async-start(), calls=%async_computation.7 | async-start | bytes 2162688 | tf_op jit(solution)/shard_map/reduce_scatter | solution.py:175
  276.9 13.1 %collective-permute-start.3 = (f32[128,2,64]{0,2,1:T(8,128)}, f32[128,2,64]{0,2,1:T(8,128)}, u32[]{:S(2)}, u32[]{:S(2)}) collective-permute-start(f32[128,2,64]{0,2,1:T(8,128)} %slice_select_fusion.2), channel_id=1, source_target_pairs={{0,4},{2,6},{4,0},{6,2},{8,12},{10,14},{12,8},{14,10},{16,20},{18,... | collective-permute-start | bytes 196616 | tf_op jit(solution)/shard_map/ppermute | solution.py:16
  292.1 3.2 collective-permute-start.4
  300.2 146.7 %all-gather.9.cloned.1.call-start = ((), (), s32[]{:S(2)}) async-start(), calls=%async_computation.8 | async-start | bytes 1081344 | tf_op jit(solution)/shard_map/all_gather | solution.py:151
  391.1 5.9 collective-permute-start.5
  397.1 187.9 %reduce-scatter.9.cloned.1.call-start = ((), (), s32[]{:S(2)}) async-start(), calls=%async_computation.9 | async-start | bytes 2162688 | tf_op jit(solution)/shard_map/reduce_scatter | solution.py:175
  471.6 13.1 %collective-permute-start.6 = (f32[128,2,64]{0,2,1:T(8,128)}, f32[128,2,64]{0,2,1:T(8,128)}, u32[]{:S(2)}, u32[]{:S(2)}) collective-permute-start(f32[128,2,64]{0,2,1:T(8,128)} %slice_select_fusion.1), channel_id=1, source_target_pairs={{0,4},{2,6},{4,0},{6,2},{8,12},{10,14},{12,8},{14,10},{16,20},{18,... | collective-permute-start | bytes 196616 | tf_op jit(solution)/shard_map/ppermute | solution.py:16
  486.8 3.2 collective-permute-start.7
  495.0 146.6 %all-gather.11.cloned.1.call-start = ((), (), s32[]{:S(2)}) async-start(), calls=%async_computation.10 | async-start | bytes 1081344 | tf_op jit(solution)/shard_map/all_gather | solution.py:151
  585.8 5.9 collective-permute-start.8
  591.7 173.3 %reduce-scatter.11.cloned.1.call-start = ((), (), s32[]{:S(2)}) async-start(), calls=%async_computation.11 | async-start | bytes 2162688 | tf_op jit(solution)/shard_map/reduce_scatter | solution.py:175
  652.0 9.6 %copy-start.11 = (f32[128,256]{1,0:T(8,128)S(1)}, f32[128,256]{1,0:T(8,128)}, u32[]{:S(2)}) copy-start(f32[128,256]{1,0:T(8,128)} %get-tuple-element.108) | copy-start | bytes 393220
  659.4 9.0 %collective-permute-start.9 = (f32[128,2,64]{0,2,1:T(8,128)}, f32[128,2,64]{0,2,1:T(8,128)}, u32[]{:S(2)}, u32[]{:S(2)}) collective-permute-start(f32[128,2,64]{0,2,1:T(8,128)} %slice_select_fusion), channel_id=1, source_target_pairs={{0,4},{2,6},{4,0},{6,2},{8,12},{10,14},{12,8},{14,10},{16,20},{18,... | collective-permute-start | bytes 196616 | tf_op jit(solution)/shard_map/ppermute | solution.py:16
  669.3 1.5 collective-permute-start.10
  674.9 90.1 %copy-start.32 = (f32[128,128]{0,1:T(8,128)S(1)}, f32[128,128]{0,1:T(8,128)}, u32[]{:S(2)}) copy-start(f32[128,128]{0,1:T(8,128)} %reduce-scatter.5.cloned.1.call-done) | copy-start | bytes 196612
  674.9 90.1 %copy-start.33 = (f32[128,128]{0,1:T(8,128)S(1)}, f32[128,128]{0,1:T(8,128)}, u32[]{:S(2)}) copy-start(f32[128,128]{0,1:T(8,128)} %reduce-scatter.7.cloned.1.call-done) | copy-start | bytes 196612
  674.9 90.1 %copy-start.34 = (f32[128,128]{0,1:T(8,128)S(1)}, f32[128,128]{0,1:T(8,128)}, u32[]{:S(2)}) copy-start(f32[128,128]{0,1:T(8,128)} %reduce-scatter.9.cloned.1.call-done) | copy-start | bytes 196612
  (74 other events, 277.3 us)
Sparse Core Ops, SparseCore 0:
  9.8 54.9 all-gather.4
  105.8 89.6 reduce-scatter.4
  202.4 49.6 all-gather.6
  300.4 89.8 reduce-scatter.6
  397.2 49.6 all-gather.8
  495.1 89.8 reduce-scatter.8
  591.8 49.7 all-gather.10
  675.0 89.9 reduce-scatter.10
where the time goes:
time: 776 us; the launch traced here: 773 us
  waiting for transfers between devices  560 us (72%)
  matrix products  80.1 us (10%)
  other arithmetic  64 us (8%)
  local copies, waits for them, and re-layouts  42 us (5%)
  between operations  15 us (2%)
  starting transfers between devices  12.4 us (2%)
    reduce_scatter x4, waiting for transfers between devices, body(): lax.psum_scatter(summed + lax.dot_general(step_rows, grad_step, (((0,), (...  360 us
    all_gather x4, waiting for transfers between devices, body(): lax.all_gather(incoming, 'tensor', axis=1, tiled=True)  189 us
    dot_general x9, matrix products, state_space(): within = jnp.einsum('hcij,cjhp->cihp', weights, scaled, precision=HIGHEST)  21.1 us
    dot_general x4, matrix products, body(): lax.dot_general(main_cols, grad_main, (((1,), (1,)), ((), ())), preferred...  20.6 us
  transfers between devices with their start and end apart: 19, of which 11 were waited for; matrix products, arithmetic and copies ran while one was open for 9% of the time, Pallas kernels for 0%

commit v1 on v0

--- a/solution.py
+++ b/solution.py
@@ -148,7 +148,10 @@
     for moment in range(sections):
         back_grad_main, back_grad_state, back_grad_step = pullback(
             lax.dot_general(
-                lax.all_gather(incoming, "tensor", axis=1, tiled=True),
+                jnp.concatenate(
+                    lax.all_to_all(jnp.stack([incoming] * lax.axis_size("tensor")), "tensor", 0, 0),
+                    axis=1,
+                ),
                 out_rows,
                 (((1,), (1,)), ((), ())),
                 preferred_element_type=jnp.float32,

time: 776 us -> 722 us (0.930); the launches traced: 773 us -> 710 us
  waiting for transfers between devices: 560 us -> 374 us
  blocking collectives: 0 us -> 108 us
  starting transfers between devices: 12.4 us -> 23.4 us
  local copies, waits for them, and re-layouts: 42 us -> 50.7 us
    all_gather x4 -> x0, waiting for transfers between devices: 189 us -> none  [body(): lax.all_gather(incoming, 'tensor', axis=1, tiled=True)]
    all_to_all x0 -> x3, blocking collectives: none -> 108 us  [body(): lax.all_to_all(jnp.stack([incoming] * lax.axis_size('tensor')), 'tensor',...]
    all_to_all x0 -> x1, waiting for transfers between devices: none -> 13.6 us  [body(): lax.all_to_all(jnp.stack([incoming] * lax.axis_size('tensor')), 'tensor',...]
    all_to_all x0 -> x1, starting transfers between devices: none -> 11.6 us  [body(): lax.all_to_all(jnp.stack([incoming] * lax.axis_size('tensor')), 'tensor',...]
    reduce_scatter x4, waiting for transfers between devices: 360 us -> 350 us  [body(): lax.psum_scatter(summed + lax.dot_general(step_rows, grad_step, (((0,), (...]
  transfers between devices with their start and end apart: 19 -> 16, of which waited for: 11 -> 8; matrix products, arithmetic and copies ran while one was open for 9% -> 10% of each run, Pallas kernels for 0% -> 0%
where the time goes in v1:
time: 722 us; the launch traced here: 710 us
  waiting for transfers between devices  374 us (52%)
  blocking collectives  108 us (15%)
  matrix products  79.1 us (11%)
  other arithmetic  59.3 us (8%)
  local copies, waits for them, and re-layouts  50.7 us (7%)
  starting transfers between devices  23.4 us (3%)
  between operations  15.3 us (2%)
    reduce_scatter x4, waiting for transfers between devices, body(): lax.psum_scatter(summed + lax.dot_general(step_rows, grad_step, (((0,), (...  350 us
    all_to_all x3, blocking collectives, body(): lax.all_to_all(jnp.stack([incoming] * lax.axis_size('tensor')), 'tensor',...  108 us
    dot_general x9, matrix products, state_space(): within = jnp.einsum('hcij,cjhp->cihp', weights, scaled, precision=HIGHEST)  20.9 us
    dot_general x4, matrix products, body(): lax.dot_general(main_cols, grad_main, (((1,), (1,)), ((), ())), preferred...  20.6 us
  transfers between devices with their start and end apart: 16, of which 8 were waited for; matrix products, arithmetic and copies ran while one was open for 10% of the time, Pallas kernels for 0%

profile of v1, /device:TPU:8, one launch (start us, length us, event | category | flops | bytes accessed | tf_op | source)
XLA Modules:
  0.0 710.0 jit_solution(17282150755682162570)
XLA Ops:
  8.8 11.6 %all-to-all-start = ((bf16[32,128,128]{1,2,0:T(8,128)(2,1)}), bf16[32,128,128]{1,2,0:T(8,128)(2,1)}, u32[]{:S(2)}, u32[]{:S(2)}) async-start(bf16[32,128,128]{1,2,0:T(8,128)(2,1)} %stack.8), calls=%async_computation | async-start | bytes 2097152 | tf_op jit(solution)/shard_map/all_to_all | solution.py:152
  32.2 4.9 copy.117
  37.1 13.6 %all-to-all-done = bf16[32,128,128]{1,2,0:T(8,128)(2,1)} async-done(((bf16[32,128,128]{1,2,0:T(8,128)(2,1)}), bf16[32,128,128]{1,2,0:T(8,128)(2,1)}, u32[]{:S(2)}, u32[]{:S(2)}) %all-to-all-start) | async-done | bytes 1048608 | tf_op jit(solution)/shard_map/all_to_all | solution.py:152
  50.7 2.1 multiply_reduce_fusion.13
  54.5 2.3 fusion.49
  59.2 2.7 fusion.63
  75.1 5.2 fusion.193
  83.1 2.5 reduce_window_sum.50
  90.7 88.6 %reduce-scatter.5.cloned.1.call-done = f32[128,128]{0,1:T(8,128)} async-done(((f32[4096,128]{0,1:T(8,128)}), f32[128,128]{0,1:T(8,128)}) %reduce-scatter.5.cloned.1.call-update) | async-done | bytes 65552 | tf_op jit(solution)/shard_map/reduce_scatter | solution.py:178
  180.1 2.6 collective-permute-start.2
  182.8 3.3 collective-permute-done.2
  188.5 36.2 %all_to_all.20 = bf16[32,128,128]{1,2,0:T(8,128)(2,1)S(1)} all-to-all(bf16[32,128,128]{1,2,0:T(8,128)(2,1)S(1)} %stack.9), channel_id=1, replica_groups=mesh['pipe'=4,'tensor'=32,'dp'=2] {'tensor'}, dimensions={0} | all-to-all | bytes 2097152 | tf_op jit(solution)/shard_map/all_to_all | solution.py:152
  228.9 2.3 fusion.51
  231.3 2.8 fusion.62
  255.6 5.2 fusion.194
  263.6 2.5 reduce_window_sum.52
  271.1 87.2 %reduce-scatter.7.cloned.1.call-done = f32[128,128]{0,1:T(8,128)} async-done(((f32[4096,128]{0,1:T(8,128)}), f32[128,128]{0,1:T(8,128)}) %reduce-scatter.7.cloned.1.call-update) | async-done | bytes 65552 | tf_op jit(solution)/shard_map/reduce_scatter | solution.py:178
  359.2 2.4 collective-permute-start.5
  361.6 3.5 collective-permute-done.5
  367.6 36.1 %all_to_all.21 = bf16[32,128,128]{1,2,0:T(8,128)(2,1)S(1)} all-to-all(bf16[32,128,128]{1,2,0:T(8,128)(2,1)S(1)} %stack.10), channel_id=1, replica_groups=mesh['pipe'=4,'tensor'=32,'dp'=2] {'tensor'}, dimensions={0} | all-to-all | bytes 2097152 | tf_op jit(solution)/shard_map/all_to_all | solution.py:152
  407.9 2.3 fusion.53
  410.2 2.8 fusion.61
  434.8 5.2 fusion.195
  442.8 2.5 reduce_window_sum.54
  450.4 87.0 %reduce-scatter.9.cloned.1.call-done = f32[128,128]{0,1:T(8,128)} async-done(((f32[4096,128]{0,1:T(8,128)}), f32[128,128]{0,1:T(8,128)}) %reduce-scatter.9.cloned.1.call-update) | async-done | bytes 65552 | tf_op jit(solution)/shard_map/reduce_scatter | solution.py:178
  538.2 2.5 collective-permute-start.8
  540.7 3.4 collective-permute-done.8
  546.6 36.1 %all_to_all.22 = bf16[32,128,128]{1,2,0:T(8,128)(2,1)S(1)} all-to-all(bf16[32,128,128]{1,2,0:T(8,128)(2,1)S(1)} %stack.11), channel_id=1, replica_groups=mesh['pipe'=4,'tensor'=32,'dp'=2] {'tensor'}, dimensions={0} | all-to-all | bytes 2097152 | tf_op jit(solution)/shard_map/all_to_all | solution.py:152
  586.3 2.3 fusion.55
  588.6 2.7 fusion.60
  602.8 5.1 fusion.196
  614.4 87.2 %reduce-scatter.11.cloned.1.call-done = f32[128,128]{0,1:T(8,128)} async-done(((f32[4096,128]{0,1:T(8,128)}), f32[128,128]{0,1:T(8,128)}) %reduce-scatter.11.cloned.1.call-update) | async-done | bytes 65552 | tf_op jit(solution)/shard_map/reduce_scatter | solution.py:178
  (376 shorter events, 138.0 us)
Async XLA Ops:
  6.5 44.2 %copy-start = (bf16[1,256,4096]{2,1,0:T(8,128)(2,1)S(1)}, bf16[1,256,4096]{2,1,0:T(8,128)(2,1)}, u32[]{:S(2)}) copy-start(bf16[1,256,4096]{2,1,0:T(8,128)(2,1)} %param.17) | copy-start | bytes 6291460
  7.6 14.8 %copy-start.81 = (f32[1,4,256]{2,1,0:T(4,128)S(1)}, f32[1,4,256]{2,1,0:T(4,128)}, u32[]{:S(2)}) copy-start(f32[1,4,256]{2,1,0:T(4,128)} %param.18) | copy-start | bytes 12292
  7.6 15.2 %copy-start.35 = (bf16[1,128,2,256]{3,2,1,0:T(2,128)(2,1)S(1)}, bf16[1,128,2,256]{3,2,1,0:T(2,128)(2,1)}, u32[]{:S(2)}) copy-start(bf16[1,128,2,256]{3,2,1,0:T(2,128)(2,1)} %param.24) | copy-start | bytes 393220
  8.8 14.2 %copy-start.94 = (f32[1,4]{1,0:T(1,128)S(1)}, f32[1,4]{1,0:T(1,128)}, u32[]{:S(2)}) copy-start(f32[1,4]{1,0:T(1,128)} %param.21) | copy-start | bytes 52
  8.8 14.3 %copy-start.46 = (bf16[1,4,128]{2,1,0:T(4,128)(2,1)S(1)}, bf16[1,4,128]{2,1,0:T(4,128)(2,1)}, u32[]{:S(2)}) copy-start(bf16[1,4,128]{2,1,0:T(4,128)(2,1)} %param.26) | copy-start | bytes 3076
  8.8 14.3 %copy-start.55 = (f32[1,4]{1,0:T(1,128)S(1)}, f32[1,4]{1,0:T(1,128)}, u32[]{:S(2)}) copy-start(f32[1,4]{1,0:T(1,128)} %param.20) | copy-start | bytes 52
  8.8 41.9 %all-to-all-start = ((bf16[32,128,128]{1,2,0:T(8,128)(2,1)}), bf16[32,128,128]{1,2,0:T(8,128)(2,1)}, u32[]{:S(2)}, u32[]{:S(2)}) async-start(bf16[32,128,128]{1,2,0:T(8,128)(2,1)} %stack.8), calls=%async_computation | async-start | bytes 2097152 | tf_op jit(solution)/shard_map/all_to_all | solution.py:152
  20.4 158.9 %reduce-scatter.5.cloned.1.call-start = ((), (), s32[]{:S(2)}) async-start(), calls=%async_computation.8 | async-start | bytes 2162688 | tf_op jit(solution)/shard_map/reduce_scatter | solution.py:178
  22.8 30.7 %copy-start.2 = (f32[128,2,256]{2,0,1:T(8,128)}, f32[128,2,256]{2,0,1:T(8,128)S(1)}, u32[]{:S(2)}) copy-start(f32[128,2,256]{2,0,1:T(8,128)S(1)} %bitcast_convert_fusion) | copy-start | bytes 786436
  23.1 14.0 %copy-start.31 = (f32[128,256]{0,1:T(8,128)}, f32[128,256]{0,1:T(8,128)S(1)}, u32[]{:S(2)}) copy-start(f32[128,256]{0,1:T(8,128)S(1)} %copy.53) | copy-start | bytes 393220
  52.9 11.9 %copy-start.6 = (f32[128,256]{1,0:T(8,128)}, f32[128,256]{1,0:T(8,128)S(1)}, u32[]{:S(2)}) copy-start(f32[128,256]{1,0:T(8,128)S(1)} %get-tuple-element.152) | copy-start | bytes 393220
  54.4 11.3 %copy-start.27 = (f32[128,256]{0,1:T(8,128)}, f32[128,256]{0,1:T(8,128)S(1)}, u32[]{:S(2)}) copy-start(f32[128,256]{0,1:T(8,128)S(1)} %copy.58) | copy-start | bytes 393220
  70.8 9.6 %collective-permute-start = (f32[128,2,64]{0,2,1:T(8,128)}, f32[128,2,64]{0,2,1:T(8,128)}, u32[]{:S(2)}, u32[]{:S(2)}) collective-permute-start(f32[128,2,64]{0,2,1:T(8,128)} %slice_select_fusion.3), channel_id=1, source_target_pairs={{0,4},{2,6},{4,0},{6,2},{8,12},{10,14},{12,8},{14,10},{16,20},{18,... | collective-permute-start | bytes 196616 | tf_op jit(solution)/shard_map/ppermute | solution.py:16
  75.0 7.4 %copy-start.60 = (f32[4,1,128]{2,1,0:T(1,128)S(1)}, f32[4,1,128]{2,1,0:T(1,128)}, u32[]{:S(2)}) copy-start(f32[4,1,128]{2,1,0:T(1,128)} %get-tuple-element.142) | copy-start | bytes 6148
  75.1 11.4 %copy-start.1 = (bf16[1,4096,2,32]{1,3,2,0:T(8,128)(2,1)S(1)}, bf16[1,4096,2,32]{1,3,2,0:T(8,128)(2,1)}, u32[]{:S(2)}) copy-start(bf16[1,4096,2,32]{1,3,2,0:T(8,128)(2,1)} %param.15) | copy-start | bytes 1572868
  82.4 3.2 collective-permute-start.1
  90.6 267.7 %reduce-scatter.7.cloned.1.call-start = ((), (), s32[]{:S(2)}) async-start(), calls=%async_computation.9 | async-start | bytes 2162688 | tf_op jit(solution)/shard_map/reduce_scatter | solution.py:178
  180.1 5.9 collective-permute-start.2
  247.6 13.2 %collective-permute-start.3 = (f32[128,2,64]{0,2,1:T(8,128)}, f32[128,2,64]{0,2,1:T(8,128)}, u32[]{:S(2)}, u32[]{:S(2)}) collective-permute-start(f32[128,2,64]{0,2,1:T(8,128)} %slice_select_fusion.2), channel_id=1, source_target_pairs={{0,4},{2,6},{4,0},{6,2},{8,12},{10,14},{12,8},{14,10},{16,20},{18,... | collective-permute-start | bytes 196616 | tf_op jit(solution)/shard_map/ppermute | solution.py:16
  262.9 3.2 collective-permute-start.4
  271.1 266.3 %reduce-scatter.9.cloned.1.call-start = ((), (), s32[]{:S(2)}) async-start(), calls=%async_computation.10 | async-start | bytes 2162688 | tf_op jit(solution)/shard_map/reduce_scatter | solution.py:178
  359.2 5.9 collective-permute-start.5
  426.6 13.5 %collective-permute-start.6 = (f32[128,2,64]{0,2,1:T(8,128)}, f32[128,2,64]{0,2,1:T(8,128)}, u32[]{:S(2)}, u32[]{:S(2)}) collective-permute-start(f32[128,2,64]{0,2,1:T(8,128)} %slice_select_fusion.1), channel_id=1, source_target_pairs={{0,4},{2,6},{4,0},{6,2},{8,12},{10,14},{12,8},{14,10},{16,20},{18,... | collective-permute-start | bytes 196616 | tf_op jit(solution)/shard_map/ppermute | solution.py:16
  442.1 3.2 collective-permute-start.7
  450.3 251.3 %reduce-scatter.11.cloned.1.call-start = ((), (), s32[]{:S(2)}) async-start(), calls=%async_computation.11 | async-start | bytes 2162688 | tf_op jit(solution)/shard_map/reduce_scatter | solution.py:178
  538.2 5.9 collective-permute-start.8
  591.3 9.7 %copy-start.11 = (f32[128,256]{1,0:T(8,128)S(1)}, f32[128,256]{1,0:T(8,128)}, u32[]{:S(2)}) copy-start(f32[128,256]{1,0:T(8,128)} %get-tuple-element.108) | copy-start | bytes 393220
  598.8 9.2 %collective-permute-start.9 = (f32[128,2,64]{0,2,1:T(8,128)}, f32[128,2,64]{0,2,1:T(8,128)}, u32[]{:S(2)}, u32[]{:S(2)}) collective-permute-start(f32[128,2,64]{0,2,1:T(8,128)} %slice_select_fusion), channel_id=1, source_target_pairs={{0,4},{2,6},{4,0},{6,2},{8,12},{10,14},{12,8},{14,10},{16,20},{18,... | collective-permute-start | bytes 196616 | tf_op jit(solution)/shard_map/ppermute | solution.py:16
  608.8 1.5 collective-permute-start.10
  614.4 87.3 %copy-start.32 = (f32[128,128]{0,1:T(8,128)S(1)}, f32[128,128]{0,1:T(8,128)}, u32[]{:S(2)}) copy-start(f32[128,128]{0,1:T(8,128)} %reduce-scatter.5.cloned.1.call-done) | copy-start | bytes 196612
  614.4 87.3 %copy-start.33 = (f32[128,128]{0,1:T(8,128)S(1)}, f32[128,128]{0,1:T(8,128)}, u32[]{:S(2)}) copy-start(f32[128,128]{0,1:T(8,128)} %reduce-scatter.7.cloned.1.call-done) | copy-start | bytes 196612
  614.4 87.3 %copy-start.34 = (f32[128,128]{0,1:T(8,128)S(1)}, f32[128,128]{0,1:T(8,128)}, u32[]{:S(2)}) copy-start(f32[128,128]{0,1:T(8,128)} %reduce-scatter.9.cloned.1.call-done) | copy-start | bytes 196612
  (79 other events, 268.8 us)
Sparse Core Ops, SparseCore 0:
  90.8 88.4 reduce-scatter.4
  271.2 87.1 reduce-scatter.6
  450.4 86.8 reduce-scatter.8
  614.5 87.0 reduce-scatter.10
